TPU v7x, 32 devices: a whole 2x2x4 slice. The times are simulated.
32 devices in a mesh: dp: 8 (over z, y), tensor: 4 (over x, core).
Axes of the slice: x: 2, y: 2, z: 4, core: 2. Of those that a mesh axis runs over, the one named last changes fastest.
Arguments:
- tokens: bfloat16 [65536, 512], P(('dp', 'tensor')), may hold values from -6 to 6
- segment_ids: int32 [128, 512], P('dp'), may hold values from 0 to 15, never falling along the last dimension, each value on 1 to 128 neighbouring positions
- row_lengths: int32 [128], P('dp'), may hold values from 256 to 512, as said below
- qkv_weight: bfloat16 [3, 512, 512], P(None, None, 'tensor'), may hold values from -6 to 6
- qv_bias: bfloat16 [2, 512], P(None, 'tensor'), may hold values from -3 to 3
- proj_weight: bfloat16 [512, 512], P('tensor'), may hold values from -6 to 6
- proj_bias: bfloat16 [512], replicated, may hold values from -3 to 3
- first_gain: bfloat16 [512], replicated, may hold values from 0.5 to 1.5
- first_shift: bfloat16 [512], replicated, may hold values from -3 to 3
- up_weight: bfloat16 [512, 2048], P(None, 'tensor'), may hold values from -6 to 6
- up_bias: bfloat16 [2048], P('tensor'), may hold values from -3 to 3
- down_weight: bfloat16 [2048, 512], P('tensor'), may hold values from -6 to 6
- down_bias: bfloat16 [512], replicated, may hold values from -3 to 3
- second_gain: bfloat16 [512], replicated, may hold values from 0.5 to 1.5
- second_shift: bfloat16 [512], replicated, may hold values from -3 to 3
- out_grad: bfloat16 [65536, 512], P(('dp', 'tensor')), may hold values from -6 to 6
Outputs:
- layer_out: bfloat16 [65536, 512], P(('dp', 'tensor'))
- tokens_grad: float32 [65536, 512], P(('dp', 'tensor'))
- qkv_weight_grad: float32 [3, 512, 512], P(None, None, 'tensor')
- qv_bias_grad: float32 [2, 512], P(None, 'tensor')
- proj_weight_grad: float32 [512, 512], P('tensor')
- proj_bias_grad: float32 [512], replicated
- first_gain_grad: float32 [512], replicated
- first_shift_grad: float32 [512], replicated
- up_weight_grad: float32 [512, 2048], P(None, 'tensor')
- up_bias_grad: float32 [2048], P('tensor')
- down_weight_grad: float32 [2048, 512], P('tensor')
- down_bias_grad: float32 [512], replicated
- second_gain_grad: float32 [512], replicated
- second_shift_grad: float32 [512], replicated
Inputs may be any that keep to these rules, and one draw needn't show every extreme that they name: `segment_ids`: ids never fall along a packed row; every id of 0 to 15 is used by 1 to 128 consecutive tokens of each row, one example of every row holding exactly 128. `row_lengths`: of the rows of one index of dp, one of the first two holds 512 tokens and the other 256; places at or past a row's length are padding.
All inputs are finite; a program needn't handle non-finite values.
Results may differ from a plain program's by a relative error of at most 0.022.
Values may be sent and summed in bfloat16 or wider, within the bound.
A program may use at most 256 MiB of HBM per device.

v0:
```python
import jax
import jax.numpy as jnp
from jax import lax
from jax.sharding import PartitionSpec as P

HEAD_DIM = 64
levels = 127.0
norm_eps = 1e-12
masked_score = -1e30


def quantize(values, peak_value):
    step_size = peak_value / levels
    scaled = values / step_size
    return (jnp.sign(scaled) * jnp.floor(jnp.abs(scaled) + 0.5), step_size)


def passes(values):
    return jnp.sign(values) * jnp.sign(values)


def exact_gelu(values):
    return jax.nn.gelu(values, approximate=False)


def group_rows(values):
    return lax.all_gather(values, "tensor", axis=0, tiled=True)


def reduce_rows(term_fn, own_rows):
    return lax.psum_scatter(
        term_fn(jnp.int32(0), lax.axis_size("tensor") * own_rows).astype(jnp.bfloat16),
        "tensor",
        scatter_dimension=0,
        tiled=True,
    ).astype(jnp.float32)


def norm_forward(values, gain_vec, shift_vec):
    centred = values - jnp.mean(values, axis=-1, keepdims=True)
    inverse = lax.rsqrt(jnp.mean(centred * centred, axis=-1, keepdims=True) + norm_eps)
    standard = centred * inverse
    return (standard * gain_vec + shift_vec, standard, inverse)


def norm_backward(incoming, standard, inverse, gain_vec):
    scaled = incoming * gain_vec
    centred = (
        scaled
        - jnp.mean(scaled, axis=-1, keepdims=True)
        - standard * jnp.mean(scaled * standard, axis=-1, keepdims=True)
    )
    return (centred * inverse, jnp.sum(incoming * standard, axis=0), jnp.sum(incoming, axis=0))


def allowed_mask(segments, lengths, seq_len):
    places = jnp.arange(seq_len)
    same_doc = segments[:, :, None] == segments[:, None, :]
    inside = places[None, None, :] < lengths[:, None, None]
    diagonal = places[:, None] == places[None, :]
    return same_doc & inside | diagonal[None]


def pair_scores(queries, keys_low, segments, lengths):
    scale_factor = queries.shape[-1] ** (-0.5)
    scores = (
        jnp.einsum("rqhe,rkhe->rhqk", queries, keys_low, preferred_element_type=jnp.float32)
        * scale_factor
    )
    allowed = allowed_mask(segments, lengths, queries.shape[1])
    return (jnp.where(allowed[:, None], scores, masked_score), scale_factor)


def attend_pair(pieces):
    queries, keys_low, values_low, segments, lengths = pieces
    scores, scale_factor = pair_scores(queries, keys_low, segments, lengths)
    top_score = jnp.max(scores, axis=-1, keepdims=True)
    weights = jnp.exp(scores - top_score)
    totals = jnp.sum(weights, axis=-1, keepdims=True)
    attn_probs = (weights / totals).astype(jnp.bfloat16)
    context = jnp.einsum(
        "rhqk,rkhe->rqhe", attn_probs, values_low, preferred_element_type=jnp.float32
    )
    return (context, top_score + jnp.log(totals))


def attend_back(pieces):
    queries, keys_low, values_low, segments, lengths, log_total, grad_context = pieces
    scores, scale_factor = pair_scores(queries, keys_low, segments, lengths)
    attn_probs = jnp.exp(scores - log_total)
    grad_values = jnp.einsum(
        "rhqk,rqhe->rkhe",
        attn_probs.astype(jnp.bfloat16),
        grad_context,
        preferred_element_type=jnp.float32,
    )
    grad_probs = jnp.einsum(
        "rqhe,rkhe->rhqk", grad_context, values_low, preferred_element_type=jnp.float32
    )
    centre = jnp.sum(grad_probs * attn_probs, axis=-1, keepdims=True)
    grad_scores = (attn_probs * (grad_probs - centre) * scale_factor).astype(jnp.bfloat16)
    grad_queries = jnp.einsum(
        "rhqk,rkhe->rqhe", grad_scores, keys_low, preferred_element_type=jnp.float32
    )
    grad_keys = jnp.einsum(
        "rhqk,rqhe->rkhe", grad_scores, queries, preferred_element_type=jnp.float32
    )
    return (grad_queries, grad_keys, grad_values)


def local(
    tokens,
    segment_ids,
    row_lengths,
    qkv_weight,
    qv_bias,
    proj_weight,
    proj_bias,
    first_gain,
    first_shift,
    up_weight,
    up_bias,
    down_weight,
    down_bias,
    second_gain,
    second_shift,
    out_grad,
):
    own_rows = tokens.shape[0]
    rows_here = segment_ids.shape[0]
    seq_len = segment_ids.shape[1]
    heads_here = qkv_weight.shape[2] // HEAD_DIM
    token_vals = tokens.astype(jnp.float32)
    qkv_vals = qkv_weight.astype(jnp.float32)
    proj_vals = proj_weight.astype(jnp.float32)
    up_vals = up_weight.astype(jnp.float32)
    down_vals = down_weight.astype(jnp.float32)
    top_qkv = jnp.max(jnp.abs(qkv_vals), axis=(1, 2))
    top_proj = jnp.max(jnp.abs(proj_vals))
    top_up = jnp.max(jnp.abs(up_vals))
    top_down = jnp.max(jnp.abs(down_vals))
    peak_qkv, peak_proj, peak_up, peak_down = lax.pmax(
        (top_qkv, top_proj, top_up, top_down), "tensor"
    )
    peak_tokens = lax.pmax(jnp.max(jnp.abs(token_vals)), ("dp", "tensor"))
    token_ints, step_tokens = quantize(token_vals, peak_tokens)
    qkv_ints, step_qkv = quantize(qkv_vals, peak_qkv[:, None, None])
    proj_ints, step_proj = quantize(proj_vals, peak_proj)
    up_ints, step_up = quantize(up_vals, peak_up)
    down_ints, step_down = quantize(down_vals, peak_down)
    qkv_low = qkv_ints.astype(jnp.bfloat16)
    proj_low = proj_ints.astype(jnp.bfloat16)
    up_low = up_ints.astype(jnp.bfloat16)
    down_low = down_ints.astype(jnp.bfloat16)
    group_tokens = group_rows(token_ints.astype(jnp.bfloat16))
    total_rows = group_tokens.shape[0]
    qkv_raw = jnp.einsum("td,idh->ith", group_tokens, qkv_low, preferred_element_type=jnp.float32)
    qkv_out = qkv_raw * (step_tokens * step_qkv)
    bias_vals = qv_bias.astype(jnp.float32)
    pair_shape = (rows_here // 2, 2, seq_len, heads_here, HEAD_DIM)
    queries = (qkv_out[0] + bias_vals[0]).astype(jnp.bfloat16).reshape(pair_shape)
    keys_low = qkv_out[1].astype(jnp.bfloat16).reshape(pair_shape)
    values_low = (qkv_out[2] + bias_vals[1]).astype(jnp.bfloat16).reshape(pair_shape)
    pair_segments = segment_ids.reshape(rows_here // 2, 2, seq_len)
    pair_lengths = row_lengths.reshape(rows_here // 2, 2)
    context_pairs, log_totals = lax.map(
        attend_pair, (queries, keys_low, values_low, pair_segments, pair_lengths)
    )
    context_low = context_pairs.reshape(total_rows, heads_here * HEAD_DIM).astype(jnp.bfloat16)

    def proj_term(row_start, row_count):
        return jnp.dot(context_low, proj_low, preferred_element_type=jnp.float32)

    proj_raw = reduce_rows(proj_term, own_rows)
    first_in = token_vals + (proj_raw * step_proj + proj_bias.astype(jnp.float32))
    first_gain_vals = first_gain.astype(jnp.float32)
    normed, first_standard, first_inverse = norm_forward(
        first_in, first_gain_vals, first_shift.astype(jnp.float32)
    )
    normed_low = normed.astype(jnp.bfloat16)
    up_full, up_bias_full, down_full = (
        lax.all_gather(up_low, "tensor", axis=1, tiled=True),
        lax.all_gather(up_bias, "tensor", axis=0, tiled=True),
        lax.all_gather(down_low, "tensor", axis=0, tiled=True),
    )
    pre_act = jnp.dot(
        normed_low, up_full, preferred_element_type=jnp.float32
    ) * step_up + up_bias_full.astype(jnp.float32)
    activated, gelu_pull = jax.vjp(exact_gelu, pre_act)
    act_low = activated.astype(jnp.bfloat16)
    down_raw = jnp.dot(act_low, down_full, preferred_element_type=jnp.float32)
    second_in = normed + (down_raw * step_down + down_bias.astype(jnp.float32))
    second_gain_vals = second_gain.astype(jnp.float32)
    layer_out, second_standard, second_inverse = norm_forward(
        second_in, second_gain_vals, second_shift.astype(jnp.float32)
    )
    grad_second, second_gain_grad, second_shift_grad = norm_backward(
        out_grad.astype(jnp.float32), second_standard, second_inverse, second_gain_vals
    )
    down_bias_grad = jnp.sum(grad_second, axis=0)
    grad_down = (grad_second * step_down).astype(jnp.bfloat16)
    down_full_grad = jnp.einsum("tf,td->fd", act_low, grad_down, preferred_element_type=jnp.float32)
    act_grad = jnp.einsum("td,fd->tf", grad_down, down_full, preferred_element_type=jnp.float32)
    (pre_grad,) = gelu_pull(act_grad)
    up_bias_full_grad = jnp.sum(pre_grad, axis=0)
    grad_up = (pre_grad * step_up).astype(jnp.bfloat16)
    up_full_grad = jnp.einsum("td,tf->df", normed_low, grad_up, preferred_element_type=jnp.float32)
    normed_back = jnp.einsum("tf,df->td", grad_up, up_full, preferred_element_type=jnp.float32)
    up_int_grad, up_bias_grad, down_int_grad = (
        lax.psum_scatter(
            up_full_grad.astype(jnp.bfloat16), "tensor", scatter_dimension=1, tiled=True
        ).astype(jnp.float32),
        lax.psum_scatter(
            up_bias_full_grad.astype(jnp.bfloat16), "tensor", scatter_dimension=0, tiled=True
        ).astype(jnp.float32),
        lax.psum_scatter(
            down_full_grad.astype(jnp.bfloat16), "tensor", scatter_dimension=0, tiled=True
        ).astype(jnp.float32),
    )
    grad_normed = grad_second + normed_back
    grad_first, first_gain_grad, first_shift_grad = norm_backward(
        grad_normed, first_standard, first_inverse, first_gain_vals
    )
    proj_bias_grad = jnp.sum(grad_first, axis=0)
    grad_proj = (grad_first * step_proj).astype(jnp.bfloat16)
    group_grad = group_rows(grad_proj)
    proj_int_grad = jnp.einsum(
        "tc,td->cd", context_low, group_grad, preferred_element_type=jnp.float32
    )
    grad_context = jnp.einsum(
        "td,cd->tc", group_grad, proj_low, preferred_element_type=jnp.float32
    ).astype(jnp.bfloat16)
    grad_pairs = lax.map(
        attend_back,
        (
            queries,
            keys_low,
            values_low,
            pair_segments,
            pair_lengths,
            log_totals,
            grad_context.reshape(pair_shape),
        ),
    )
    grad_queries = grad_pairs[0].reshape(total_rows, heads_here * HEAD_DIM)
    grad_keys = grad_pairs[1].reshape(total_rows, heads_here * HEAD_DIM)
    grad_values = grad_pairs[2].reshape(total_rows, heads_here * HEAD_DIM)
    qv_bias_grad = jnp.stack([jnp.sum(grad_queries, axis=0), jnp.sum(grad_values, axis=0)])
    grad_qkv = (
        jnp.stack([grad_queries, grad_keys, grad_values]) * (step_tokens * step_qkv)
    ).astype(jnp.bfloat16)
    qkv_int_grad = jnp.einsum(
        "td,ith->idh", group_tokens, grad_qkv, preferred_element_type=jnp.float32
    )

    def input_term(row_start, row_count):
        return jnp.einsum("ith,idh->td", grad_qkv, qkv_low, preferred_element_type=jnp.float32)

    token_int_grad = reduce_rows(input_term, own_rows)
    tokens_grad = grad_first + token_int_grad * passes(token_vals) / step_tokens
    shard_sums = (
        lax.psum(qkv_int_grad.astype(jnp.bfloat16), "dp").astype(jnp.float32),
        lax.psum(qv_bias_grad.astype(jnp.bfloat16), "dp").astype(jnp.float32),
        lax.psum(proj_int_grad.astype(jnp.bfloat16), "dp").astype(jnp.float32),
        lax.psum(up_int_grad.astype(jnp.bfloat16), "dp").astype(jnp.float32),
        lax.psum(up_bias_grad.astype(jnp.bfloat16), "dp").astype(jnp.float32),
        lax.psum(down_int_grad.astype(jnp.bfloat16), "dp").astype(jnp.float32),
    )
    common_sums = lax.psum(
        (
            proj_bias_grad,
            first_gain_grad,
            first_shift_grad,
            down_bias_grad,
            second_gain_grad,
            second_shift_grad,
        ),
        ("dp", "tensor"),
    )
    return (
        layer_out.astype(jnp.bfloat16),
        tokens_grad,
        shard_sums[0] * passes(qkv_vals) / step_qkv,
        shard_sums[1],
        shard_sums[2] * passes(proj_vals) / step_proj,
        common_sums[0],
        common_sums[1],
        common_sums[2],
        shard_sums[3] * passes(up_vals) / step_up,
        shard_sums[4],
        shard_sums[5] * passes(down_vals) / step_down,
        common_sums[3],
        common_sums[4],
        common_sums[5],
    )


def solution(mesh):
    in_specs = (
        P(("dp", "tensor"), None),
        P("dp", None),
        P("dp"),
        P(None, None, "tensor"),
        P(None, "tensor"),
        P("tensor", None),
        P(),
        P(),
        P(),
        P(None, "tensor"),
        P("tensor"),
        P("tensor", None),
        P(),
        P(),
        P(),
        P(("dp", "tensor"), None),
    )
    out_specs = (
        P(("dp", "tensor"), None),
        P(("dp", "tensor"), None),
        P(None, None, "tensor"),
        P(None, "tensor"),
        P("tensor", None),
        P(),
        P(),
        P(),
        P(None, "tensor"),
        P("tensor"),
        P("tensor", None),
        P(),
        P(),
        P(),
    )
    return jax.shard_map(local, mesh=mesh, in_specs=in_specs, out_specs=out_specs, check_vma=False)
```

profile of v0, /device:TPU:0, one launch (start us, length us, event | category | flops | bytes accessed | tf_op | source)
XLA Modules:
  0.0 994.4 jit_solution(8438317445170648339)
XLA Ops:
  9.8 42.2 %pmax.36 = f32[]{:T(128)} all-reduce(f32[]{:T(128)} %fusion.88), channel_id=1, replica_groups=mesh['dp'=8,'tensor'=4] {'dp','tensor'}, use_global_device_ids=true, to_apply=%region_3.0 | all-reduce | flops 1 | bytes 8 | tf_op jit(solution)/shard_map/pmax | solution.py:145
  59.2 6.6 all-reduce.2
  69.5 46.4 %all-gather.6.cloned.1.call-done = bf16[8192,512]{1,0:T(8,128)(2,1)} async-done(((bf16[2048,512]{1,0:T(8,128)(2,1)}), bf16[8192,512]{1,0:T(8,128)(2,1)}) %all-gather.6.cloned.1.call-update) | async-done | bytes 8388624 | tf_op jit(solution)/shard_map/all_gather | solution.py:27
  115.9 6.2 multiply_bitcast_fusion
  127.6 6.6 squeeze.37
  134.2 6.6 squeeze.38
  156.7 59.9 %while.28 = (s32[]{:T(128)}, bf16[8,2,512,2,64]{2,4,3,1,0:T(8,128)(2,1)S(1)}, f32[8,2,2,512,1]{3,2,1,4,0:T(2,128)}, bf16[8,2,512,2,64]{2,4,3,1,0:T(8,128)(2,1)},...) while((s32[]{:T(128)}, ...), condition=%wide.region_7.0_spmd.clone, body=%wide.region_4.7_spmd.sunk.clone | while | flops 282852352 | bytes 16597121 | solution.py:166
  238.7 62.4 %reduce-scatter.5.cloned.1.call-done = bf16[2048,512]{1,0:T(8,128)(2,1)} async-done(((bf16[8192,512]{1,0:T(8,128)(2,1)}), bf16[2048,512]{1,0:T(8,128)(2,1)}) %reduce-scatter.5.cloned.1.call-update) | async-done | bytes 2097168 | tf_op jit(solution)/shard_map/reduce_scatter | solution.py:31
  305.1 20.9 %all-gather.8.cloned.1.call-done = bf16[512,2048]{1,0:T(8,128)(2,1)} async-done(((bf16[512,512]{1,0:T(8,128)(2,1)}), bf16[512,2048]{1,0:T(8,128)(2,1)}) %all-gather.8.cloned.1.call-update) | async-done | bytes 2097168 | tf_op jit(solution)/shard_map/all_gather | solution.py:182
  325.9 45.9 %multiply_convert_fusion.2 = (bf16[2048,2048]{1,0:T(8,128)(2,1)}, f32[2048,2048]{1,0:T(8,128)}, f32[2048,2048]{1,0:T(8,128)}) fusion(f32[2048]{0:T(1024)S(1)} %bitcast.166, f32[]{:T(128)S(6)} %div.112, bf16[512,2048]{1,0:T(8,128)(2,1)} %all-gather.8.cloned.1.call-done, f32[512]{0:T(512)S(1)} %convert_element_type.180, f32[512]{0:T(512)S(1)} %convert_element_type.179, ...), kind=kOutput, calls=%fused_computation.79 | convolution fusion | flops 4586471424 | bytes 48265224 | tf_op jit(solution)/shard_map/dot_general | solution.py:186
  371.9 9.0 fusion.133
  390.3 22.4 %fusion.134 = (bf16[2048]{0:T(1024)(128)(2,1)S(1)}, f32[2048,2048]{1,0:T(8,128)}) fusion(f32[2048,2048]{1,0:T(8,128)} %get-tuple-element.289, bf16[2048,512]{1,0:T(8,128)(2,1)} %all-gather.10.cloned.1.call-done, f32[2048,512]{1,0:T(8,128)} %get-tuple-element.285, f32[]{:T(128)S(6)} %div.115, f32[2048]{0:T(1024)S(1)} %bitcast.167, ...), kind=kOutput, calls=%fused_computation.200 | convolution fusion | flops 4364171264 | bytes 56635400 | tf_op jit(solution)/shard_map/td,fd->tf/dot_general | solution.py:203
  412.7 11.7 %multiply_reduce_fusion.1 = (f32[512]{0:T(512)S(1)}, f32[2048]{0:T(1024)S(1)}, f32[2048]{0:T(1024)S(1)}, f32[512]{0:T(512)S(1)}, f32[2048,512]{1,0:T(8,128)S(1)}) fusion(f32[2048]{0:T(1024)S(1)} %add_rsqrt_fusion.1, f32[2048]{0:T(1024)S(1)} %broadcast_multiply_fusion.5, f32[512]{0:T(512)S(1)} %convert_element_type.178, f32[]{:T(128)S(6)} %div.107, ...), kind=kOutput, calls=%fused_computation.126 | convolution fusion | flops 4319079424 | bytes 31498248 | tf_op jit(solution)/shard_map/tf,df->td/dot_general | solution.py:208
  430.8 13.4 %fusion.99 = bf16[512,2048]{1,0:T(8,128)(2,1)} fusion(f32[2048,2048]{1,0:T(8,128)} %get-tuple-element.302, f32[]{:T(128)S(6)} %div.112, f32[512]{0:T(512)S(1)} %convert_element_type.180, f32[512]{0:T(512)S(1)} %convert_element_type.179, bf16[2048,512]{1,0:T(8,128)(2,1)} %reduce-scatter.5.cloned.1.call-done, bf16[2048,512]{1,0:T(8,128)(2,1)S(1)} %copy-done, ...), kind=kOutput, calls=%fused_computation.145 | convolution fusion | flops 4314890240 | bytes 23091208 | tf_op jit(solution)/shard_map/td,tf->df/dot_general | solution.py:207
  444.3 10.5 %convolution_convert_fusion.2 = bf16[2048,512]{1,0:T(8,128)(2,1)} fusion(bf16[2048,2048]{1,0:T(8,128)(2,1)} %get-tuple-element.288, f32[2048,512]{1,0:T(8,128)} %get-tuple-element.285, f32[]{:T(128)S(6)} %div.115), kind=kOutput, calls=%fused_computation.144 | convolution fusion | flops 4298113024 | bytes 14680068 | tf_op jit(solution)/shard_map/tf,td->fd/dot_general | solution.py:202
  454.9 34.1 %all-gather.12.cloned.1.call-done = bf16[8192,512]{1,0:T(8,128)(2,1)} async-done(((bf16[2048,512]{1,0:T(8,128)(2,1)}), bf16[8192,512]{1,0:T(8,128)(2,1)}) %all-gather.12.cloned.1.call-update) | async-done | bytes 8388624 | tf_op jit(solution)/shard_map/all_gather | solution.py:27
  489.0 7.1 convolution_convert_fusion.1
  496.1 8.6 reshape.233
  504.8 10.6 %copy.72 = bf16[8,2,512,2,64]{2,4,3,1,0:T(8,128)(2,1)} copy(bf16[8,2,512,2,64]{4,3,2,1,0:T(2,128)(2,1)} %reshape.233) | data formatting | bytes 4194304 | tf_op jit(solution)/shard_map/while | solution.py:233
  515.4 250.8 %while.29 = (s32[]{:T(128)}, f32[8,2,512,2,64]{2,4,3,1,0:T(8,128)}, f32[8,2,512,2,64]{2,1,0,4,3:T(2,128)}, f32[8,2,512,2,64]{2,4,3,1,0:T(8,128)}, bf16[8,2,512,2...) while((s32[]{:T(128)}, f32[8,2,512,2,64]{2,4,3,1,0:T(8,128)}, ...), condition=%wide.region_25.26_spmd.clone, body=%wide.region_23.25_spmd.sunk.clone | while | flops 687609856 | bytes 52209824 | solution.py:233
  526.4 8.4 fusion.202
  534.8 7.2 fusion.203
  558.2 8.1 fusion.202
  566.3 7.1 fusion.203
  589.6 8.0 fusion.202
  597.6 7.1 fusion.203
  620.8 8.0 fusion.202
  628.8 7.1 fusion.203
  652.1 8.1 fusion.202
  660.1 7.1 fusion.203
  683.4 8.1 fusion.202
  691.4 7.1 fusion.203
  714.7 8.0 fusion.202
  722.7 7.1 fusion.203
  745.9 8.0 fusion.202
  753.9 7.1 fusion.203
  766.2 7.4 copy.75
  773.6 6.6 stack_reshape.11
  780.2 6.8 stack_reshape.10
  786.9 7.3 copy.73
  794.3 6.6 stack_reshape.9
  808.7 7.6 fusion.104
  816.4 10.3 %bitcast_convert_fusion = bf16[8192,512]{1,0:T(8,128)(2,1)} fusion(bf16[3,512,128]{1,2,0:T(8,128)(2,1)S(1)} %copy-done.9, f32[3]{0:T(128)S(1)} %copy-done.23, f32[1,8192,128]{1,2,0:T(8,128)} %stack_reshape.11, f32[1,8192,128]{1,2,0:T(8,128)} %stack_reshape.10, f32[1,8192,128]{1,2,0:T(8,128)} %stack_reshape.9, f32[3]{0:T(128)S(1)} %copy-done.27), kind=kOutput, calls=%fused_computation.76 | convolution fusion | flops 3239575552 | bytes 21364760 | tf_op jit(solution)/shard_map/ith,idh->td/dot_general | solution.py:257
  828.5 6.5 all-reduce
  835.1 40.9 %all-reduce.1 = (f32[512]{0:T(512)}, f32[512]{0:T(512)}, f32[512]{0:T(512)}, f32[512]{0:T(512)}, f32[512]{0:T(512)}, /*index=5*/f32[512]{0:T(512)}) all-reduce(f32[512]{0:T(512)S(1)} %get-tuple-element.286, f32[512]{0:T(512)S(1)} %get-tuple-element.220, ...), channel_id=1, replica_groups=mesh['dp'=8,'tensor'=4] {'dp','tensor'}, use_global_device_ids=true, to_apply=%region_33.34 | all-reduce | flops 3072 | bytes 24576 | tf_op jit(solution)/shard_map/psum | solution.py:269
  882.5 22.2 %all-reduce.3 = (bf16[2,128]{1,0:T(2,128)(2,1)}, bf16[512]{0:T(512)(128)(2,1)S(1)}) all-reduce(bf16[2,128]{1,0:T(2,128)(2,1)S(1)} %pad_maximum_fusion, bf16[512]{0:T(512)(128)(2,1)S(1)} %dynamic-slice.1), channel_id=1, replica_groups=mesh['dp'=8,'tensor'=4] {'dp'}, use_global_device_ids=true, to_apply=%region_30.31 | all-reduce | flops 768 | bytes 3072 | tf_op jit(solution)/shard_map/psum | solution.py:263
  918.1 62.9 %reduce-scatter.7.cloned.1.call-done = bf16[2048,512]{1,0:T(8,128)(2,1)} async-done(((bf16[8192,512]{1,0:T(8,128)(2,1)}), bf16[2048,512]{1,0:T(8,128)(2,1)}) %reduce-scatter.7.cloned.1.call-update) | async-done | bytes 2097168 | tf_op jit(solution)/shard_map/reduce_scatter | solution.py:31
  981.0 6.6 fusion.92
  (324 shorter events, 290.3 us)
Async XLA Ops:
  7.2 50.3 %copy-start.20 = (bf16[3,512,128]{2,1,0:T(8,128)(2,1)S(1)}, bf16[3,512,128]{2,1,0:T(8,128)(2,1)}, u32[]{:S(2)}) copy-start(bf16[3,512,128]{2,1,0:T(8,128)(2,1)} %param.23) | copy-start | bytes 1179652
  7.2 50.5 %copy-start.17 = (bf16[128,512]{1,0:T(8,128)(2,1)S(1)}, bf16[128,512]{1,0:T(8,128)(2,1)}, u32[]{:S(2)}) copy-start(bf16[128,512]{1,0:T(8,128)(2,1)} %param.25) | copy-start | bytes 393220
  7.2 108.7 %all-gather.6.cloned.1.call-start = ((), (), s32[]{:S(2)}) async-start(), calls=%async_computation.4 | async-start | bytes 10485760 | tf_op jit(solution)/shard_map/all_gather | solution.py:27
  9.8 48.7 %copy-start.10 = (bf16[512,512]{1,0:T(8,128)(2,1)S(1)}, bf16[512,512]{1,0:T(8,128)(2,1)}, u32[]{:S(2)}) copy-start(bf16[512,512]{1,0:T(8,128)(2,1)} %param.29) | copy-start | bytes 1572868
  9.8 48.7 %copy-start.12 = (bf16[512,512]{1,0:T(8,128)(2,1)S(1)}, bf16[512,512]{1,0:T(8,128)(2,1)}, u32[]{:S(2)}) copy-start(bf16[512,512]{1,0:T(8,128)(2,1)} %param.31) | copy-start | bytes 1572868
  52.6 13.9 %copy-start.39 = (bf16[2,128]{1,0:T(2,128)(2,1)S(1)}, bf16[2,128]{1,0:T(2,128)(2,1)}, u32[]{:S(2)}) copy-start(bf16[2,128]{1,0:T(2,128)(2,1)} %param.24) | copy-start | bytes 1540
  52.6 14.0 %copy-start.21 = (s32[16,512]{1,0:T(8,128)S(1)}, s32[16,512]{1,0:T(8,128)}, u32[]{:S(2)}) copy-start(s32[16,512]{1,0:T(8,128)} %param.21) | copy-start | bytes 98308
  52.6 14.6 %copy-start.38 = (s32[16]{0:T(128)S(1)}, s32[16]{0:T(128)}, u32[]{:S(2)}) copy-start(s32[16]{0:T(128)} %param.22) | copy-start | bytes 196
  57.4 243.7 %reduce-scatter.5.cloned.1.call-start = ((), (), s32[]{:S(2)}) async-start(), calls=%async_computation.5 | async-start | bytes 10485760 | tf_op jit(solution)/shard_map/reduce_scatter | solution.py:31
  57.7 64.4 %copy-start.8 = (bf16[3,512,128]{1,2,0:T(8,128)(2,1)}, bf16[3,512,128]{1,2,0:T(8,128)(2,1)S(1)}, u32[]{:S(2)}) copy-start(bf16[3,512,128]{1,2,0:T(8,128)(2,1)S(1)} %copy.65) | copy-start | bytes 1179652
  69.5 52.6 %copy-start.22 = (f32[3]{0:T(128)}, f32[3]{0:T(128)S(1)}, u32[]{:S(2)}) copy-start(f32[3]{0:T(128)S(1)} %get-tuple-element.295) | copy-start | bytes 40
  69.5 52.6 %copy-start.26 = (f32[3]{0:T(128)}, f32[3]{0:T(128)S(1)}, u32[]{:S(2)}) copy-start(f32[3]{0:T(128)S(1)} %get-tuple-element.296) | copy-start | bytes 40
  145.2 4.2 copy-start.5
  149.5 3.6 copy-start.6
  149.5 3.6 copy-start.37
  216.6 6.8 copy-start.29
  216.6 6.8 copy-start.18
  223.4 5.7 copy-start.2
  229.1 4.2 copy-start.30
  229.1 4.3 copy-start.31
  229.1 9.5 copy-start.32
  229.1 9.5 copy-start.33
  229.1 9.5 copy-start.34
  229.1 9.5 copy-start.35
  229.1 9.5 copy-start.36
  229.1 71.9 %copy-start = (bf16[2048,512]{1,0:T(8,128)(2,1)S(1)}, bf16[2048,512]{1,0:T(8,128)(2,1)}, u32[]{:S(2)}) copy-start(bf16[2048,512]{1,0:T(8,128)(2,1)} %param.20) | copy-start | bytes 6291460
  229.2 96.8 %all-gather.8.cloned.1.call-start = ((), (), s32[]{:S(2)}) async-start(), calls=%async_computation.6 | async-start | bytes 2621440 | tf_op jit(solution)/shard_map/all_gather | solution.py:182
  231.3 140.6 %all-gather.10.cloned.1.call-start = ((), (), s32[]{:S(2)}) async-start(), calls=%async_computation.7 | async-start | bytes 2621440 | tf_op jit(solution)/shard_map/all_gather | solution.py:184
  233.3 255.7 %all-gather.12.cloned.1.call-start = ((), (), s32[]{:S(2)}) async-start(), calls=%async_computation.8 | async-start | bytes 10485760 | tf_op jit(solution)/shard_map/all_gather | solution.py:27
  301.1 2.6 copy-start.3
  412.7 11.7 %copy-start.4 = (bf16[2048,512]{1,0:T(8,128)(2,1)S(1)}, bf16[2048,512]{1,0:T(8,128)(2,1)}, u32[]{:S(2)}) copy-start(bf16[2048,512]{1,0:T(8,128)(2,1)} %reduce-scatter.5.cloned.1.call-done) | copy-start | bytes 6291460
  426.7 2.0 copy-start.1
  430.6 385.7 %reduce-scatter.9.cloned.1.call-start = ((), (), s32[]{:S(2)}) async-start(), calls=%async_computation.10 | async-start | bytes 2621440 | tf_op jit(solution)/shard_map/reduce_scatter | solution.py:210
  444.2 372.1 %reduce-scatter.11.cloned.1.call-start = ((), (), s32[]{:S(2)}) async-start(), calls=%async_computation.11 | async-start | bytes 2621440 | tf_op jit(solution)/shard_map/reduce_scatter | solution.py:216
  444.3 44.7 %copy-start.19 = (bf16[128,512]{1,0:T(8,128)(2,1)S(1)}, bf16[128,512]{1,0:T(8,128)(2,1)}, u32[]{:S(2)}) copy-start(bf16[128,512]{1,0:T(8,128)(2,1)} %param.25) | copy-start | bytes 393220
  454.8 452.2 %all-reduce.7.cloned.1.call-start = ((), (), s32[]{:S(2)}) async-start(), calls=%async_computation.12 | async-start | bytes 3145728 | tf_op jit(solution)/shard_map/psum | solution.py:262
  800.9 6.1 copy-start.14
  800.9 6.5 copy-start.15
  800.9 7.7 copy-start.16
  800.9 7.7 copy-start.27
  808.7 7.7 copy-start.9
  808.7 7.7 copy-start.23
  816.3 164.7 %reduce-scatter.7.cloned.1.call-start = ((), (), s32[]{:S(2)}) async-start(), calls=%async_computation.9 | async-start | bytes 10485760 | tf_op jit(solution)/shard_map/reduce_scatter | solution.py:31
  826.6 8.5 copy-start.24
  826.6 8.5 copy-start.25
  826.7 8.5 copy-start.28
  878.5 34.7 %copy-start.11 = (bf16[512,512]{1,0:T(8,128)(2,1)S(1)}, bf16[512,512]{1,0:T(8,128)(2,1)}, u32[]{:S(2)}) copy-start(bf16[512,512]{1,0:T(8,128)(2,1)} %param.29) | copy-start | bytes 1572868
  878.5 37.1 %copy-start.13 = (bf16[512,512]{1,0:T(8,128)(2,1)S(1)}, bf16[512,512]{1,0:T(8,128)(2,1)}, u32[]{:S(2)}) copy-start(bf16[512,512]{1,0:T(8,128)(2,1)} %param.31) | copy-start | bytes 1572868
  (2 other events, 2.2 us)
Sparse Core Ops, SparseCore 0:
  57.6 58.2 all-gather.5
  229.3 71.7 reduce-scatter.4
  303.3 22.5 all-gather.7
  328.0 22.5 all-gather.9
  430.7 58.2 all-gather.11
  491.5 31.4 reduce-scatter.8
  525.5 31.4 reduce-scatter.10
  816.4 90.5 all-reduce.6
  909.8 71.1 reduce-scatter.6
where the time goes:
time: 1000 us; the launch traced here: 994 us
  matrix products  409 us (41%)
  waiting for transfers between devices  227 us (23%)
  local copies, waits for them, and re-layouts  131 us (13%)
  blocking collectives  124 us (12%)
  other arithmetic  84.1 us (8%)
  between operations  18.7 us (2%)
    reduce_scatter x2, waiting for transfers between devices, reduce_rows(): lax.psum_scatter(term_fn(jnp.int32(0), lax.axis_size('tensor') * own_rows...  125 us
    all_gather x2, waiting for transfers between devices, group_rows(): return lax.all_gather(values, 'tensor', axis=0, tiled=True)  80.5 us
    dot_general x8, matrix products, attend_back(): jnp.einsum('rhqk,rkhe->rqhe', grad_scores, keys_low, preferred_element_ty...  64.8 us
    dot_general x8, matrix products, attend_back(): jnp.einsum('rhqk,rqhe->rkhe', grad_scores, queries, preferred_element_typ...  57 us
    dot_general x16, matrix products, pair_scores(): jnp.einsum('rqhe,rkhe->rhqk', queries, keys_low, preferred_element_type=j...  51.8 us
    dot_general x1, matrix products, local(): jnp.dot(normed_low, up_full, preferred_element_type=jnp.float32) * step_up  45.9 us
    pmax x1, blocking collectives, local(): peak_tokens = lax.pmax(jnp.max(jnp.abs(token_vals)), ('dp', 'tensor'))  42.2 us
    psum x1, blocking collectives, local(): lax.psum((proj_bias_grad, first_gain_grad, first_shift_grad, down_bias_gr...  40.9 us
  transfers between devices with their start and end apart: 9, of which 6 were waited for; matrix products, arithmetic and copies ran while one was open for 44% of the time, Pallas kernels for 0%

commit v1 on v0

--- a/solution.py
+++ b/solution.py
@@ -267,15 +267,18 @@
         lax.psum(down_int_grad.astype(jnp.bfloat16), "dp").astype(jnp.float32),
     )
     common_sums = lax.psum(
-        (
-            proj_bias_grad,
-            first_gain_grad,
-            first_shift_grad,
-            down_bias_grad,
-            second_gain_grad,
-            second_shift_grad,
+        lax.psum(
+            (
+                proj_bias_grad,
+                first_gain_grad,
+                first_shift_grad,
+                down_bias_grad,
+                second_gain_grad,
+                second_shift_grad,
+            ),
+            "tensor",
         ),
-        ("dp", "tensor"),
+        "dp",
     )
     return (
         layer_out.astype(jnp.bfloat16),

time: 1000 us -> 1000 us (level)
    psum x0 -> x1, blocking collectives: none -> 37.4 us  [local(): lax.psum(lax.psum((proj_bias_grad, first_gain_grad, first_shift_grad, dow...]
    psum x1, blocking collectives: 40.9 us -> 10.7 us  [local(): lax.psum((proj_bias_grad, first_gain_grad, first_shift_grad, down_bias_gr...]
  transfers between devices with their start and end apart: 9 -> 9, of which waited for: 6 -> 5; matrix products, arithmetic and copies ran while one was open for 44% -> 44% of each run, Pallas kernels for 0% -> 0%
where the time goes in v1:
time: 1000 us; the launch traced here: 993 us
  matrix products  415 us (42%)
  waiting for transfers between devices  224 us (22%)
  blocking collectives  127 us (13%)
  local copies, waits for them, and re-layouts  122 us (12%)
  other arithmetic  85.4 us (9%)
  between operations  18.7 us (2%)
    reduce_scatter x2, waiting for transfers between devices, reduce_rows(): lax.psum_scatter(term_fn(jnp.int32(0), lax.axis_size('tensor') * own_rows...  122 us
    all_gather x2, waiting for transfers between devices, group_rows(): return lax.all_gather(values, 'tensor', axis=0, tiled=True)  80.9 us
    dot_general x8, matrix products, attend_back(): jnp.einsum('rhqk,rkhe->rqhe', grad_scores, keys_low, preferred_element_ty...  64.8 us
    dot_general x8, matrix products, attend_back(): jnp.einsum('rhqk,rqhe->rkhe', grad_scores, queries, preferred_element_typ...  57 us
    dot_general x16, matrix products, pair_scores(): jnp.einsum('rqhe,rkhe->rhqk', queries, keys_low, preferred_element_type=j...  51.8 us
    dot_general x1, matrix products, local(): jnp.dot(normed_low, up_full, preferred_element_type=jnp.float32) * step_up  46 us
    pmax x1, blocking collectives, local(): peak_tokens = lax.pmax(jnp.max(jnp.abs(token_vals)), ('dp', 'tensor'))  42.2 us
    psum x1, blocking collectives, local(): lax.psum(lax.psum((proj_bias_grad, first_gain_grad, first_shift_grad, dow...  37.4 us
  transfers between devices with their start and end apart: 9, of which 5 were waited for; matrix products, arithmetic and copies ran while one was open for 44% of the time, Pallas kernels for 0%

profile of v1, /device:TPU:0, one launch (start us, length us, event | category | flops | bytes accessed | tf_op | source)
XLA Modules:
  0.0 993.1 jit_solution(2691219919417635453)
XLA Ops:
  9.8 42.2 %pmax.36 = f32[]{:T(128)} all-reduce(f32[]{:T(128)} %fusion.88), channel_id=1, replica_groups=mesh['dp'=8,'tensor'=4] {'dp','tensor'}, use_global_device_ids=true, to_apply=%region_3.0 | all-reduce | flops 1 | bytes 8 | tf_op jit(solution)/shard_map/pmax | solution.py:145
  59.2 6.6 all-reduce.3
  69.1 46.8 %all-gather.6.cloned.1.call-done = bf16[8192,512]{1,0:T(8,128)(2,1)} async-done(((bf16[2048,512]{1,0:T(8,128)(2,1)}), bf16[8192,512]{1,0:T(8,128)(2,1)}) %all-gather.6.cloned.1.call-update) | async-done | bytes 8388624 | tf_op jit(solution)/shard_map/all_gather | solution.py:27
  126.3 6.6 squeeze.37
  132.9 6.6 squeeze.38
  153.6 60.1 %while.28 = (s32[]{:T(128)}, bf16[8,2,512,2,64]{2,4,3,1,0:T(8,128)(2,1)}, f32[8,2,2,512,1]{3,2,1,4,0:T(2,128)}, bf16[8,2,512,2,64]{2,4,3,1,0:T(8,128)(2,1)}, s32...) while((s32[]{:T(128)}, ...), condition=%wide.region_7.0_spmd.clone, body=%wide.region_4.7_spmd.sunk.clone | while | flops 282852352 | bytes 16597121 | solution.py:166
  237.4 62.4 %reduce-scatter.5.cloned.1.call-done = bf16[2048,512]{1,0:T(8,128)(2,1)} async-done(((bf16[8192,512]{1,0:T(8,128)(2,1)}), bf16[2048,512]{1,0:T(8,128)(2,1)}) %reduce-scatter.5.cloned.1.call-update) | async-done | bytes 2097168 | tf_op jit(solution)/shard_map/reduce_scatter | solution.py:31
  303.8 20.9 %all-gather.8.cloned.1.call-done = bf16[512,2048]{1,0:T(8,128)(2,1)} async-done(((bf16[512,512]{1,0:T(8,128)(2,1)}), bf16[512,2048]{1,0:T(8,128)(2,1)}) %all-gather.8.cloned.1.call-update) | async-done | bytes 2097168 | tf_op jit(solution)/shard_map/all_gather | solution.py:182
  324.6 46.0 %multiply_convert_fusion.2 = (bf16[2048,2048]{1,0:T(8,128)(2,1)}, f32[2048,2048]{1,0:T(8,128)}, f32[2048,2048]{1,0:T(8,128)}) fusion(f32[2048]{0:T(1024)S(1)} %bitcast.166, f32[]{:T(128)S(6)} %div.112, bf16[512,2048]{1,0:T(8,128)(2,1)} %all-gather.8.cloned.1.call-done, f32[512]{0:T(512)S(1)} %convert_element_type.180, f32[512]{0:T(512)S(1)} %convert_element_type.179, ...), kind=kOutput, calls=%fused_computation.79 | convolution fusion | flops 4586471424 | bytes 48265224 | tf_op jit(solution)/shard_map/dot_general | solution.py:186
  370.6 9.0 fusion.133
  389.0 22.4 %fusion.134 = (bf16[2048]{0:T(1024)(128)(2,1)S(1)}, f32[2048,2048]{1,0:T(8,128)}) fusion(f32[2048,2048]{1,0:T(8,128)} %get-tuple-element.295, bf16[2048,512]{1,0:T(8,128)(2,1)} %all-gather.10.cloned.1.call-done, f32[2048,512]{1,0:T(8,128)} %get-tuple-element.291, f32[]{:T(128)S(6)} %div.115, f32[2048]{0:T(1024)S(1)} %bitcast.167, ...), kind=kOutput, calls=%fused_computation.200 | convolution fusion | flops 4364171264 | bytes 56635400 | tf_op jit(solution)/shard_map/td,fd->tf/dot_general | solution.py:203
  411.4 11.7 %multiply_reduce_fusion.1 = (f32[512]{0:T(512)S(1)}, f32[2048]{0:T(1024)S(1)}, f32[2048]{0:T(1024)S(1)}, f32[512]{0:T(512)S(1)}, f32[2048,512]{1,0:T(8,128)S(1)}) fusion(f32[2048]{0:T(1024)S(1)} %add_rsqrt_fusion.1, f32[2048]{0:T(1024)S(1)} %broadcast_multiply_fusion.5, f32[512]{0:T(512)S(1)} %convert_element_type.178, f32[]{:T(128)S(6)} %div.107, ...), kind=kOutput, calls=%fused_computation.126 | convolution fusion | flops 4319079424 | bytes 31498248 | tf_op jit(solution)/shard_map/tf,df->td/dot_general | solution.py:208
  429.6 13.4 %fusion.99 = bf16[512,2048]{1,0:T(8,128)(2,1)} fusion(f32[2048,2048]{1,0:T(8,128)} %get-tuple-element.308, f32[]{:T(128)S(6)} %div.112, f32[512]{0:T(512)S(1)} %convert_element_type.180, f32[512]{0:T(512)S(1)} %convert_element_type.179, bf16[2048,512]{1,0:T(8,128)(2,1)} %reduce-scatter.5.cloned.1.call-done, bf16[2048,512]{1,0:T(8,128)(2,1)S(1)} %copy-done, ...), kind=kOutput, calls=%fused_computation.145 | convolution fusion | flops 4314890240 | bytes 23091208 | tf_op jit(solution)/shard_map/td,tf->df/dot_general | solution.py:207
  443.1 10.5 %convolution_convert_fusion.2 = bf16[2048,512]{1,0:T(8,128)(2,1)} fusion(bf16[2048,2048]{1,0:T(8,128)(2,1)} %get-tuple-element.294, f32[2048,512]{1,0:T(8,128)} %get-tuple-element.291, f32[]{:T(128)S(6)} %div.115), kind=kOutput, calls=%fused_computation.144 | convolution fusion | flops 4298113024 | bytes 14680068 | tf_op jit(solution)/shard_map/tf,td->fd/dot_general | solution.py:202
  453.6 34.1 %all-gather.12.cloned.1.call-done = bf16[8192,512]{1,0:T(8,128)(2,1)} async-done(((bf16[2048,512]{1,0:T(8,128)(2,1)}), bf16[8192,512]{1,0:T(8,128)(2,1)}) %all-gather.12.cloned.1.call-update) | async-done | bytes 8388624 | tf_op jit(solution)/shard_map/all_gather | solution.py:27
  487.8 7.1 convolution_convert_fusion.1
  494.9 8.6 reshape.233
  503.5 10.6 %copy.72 = bf16[8,2,512,2,64]{2,4,3,1,0:T(8,128)(2,1)} copy(bf16[8,2,512,2,64]{4,3,2,1,0:T(2,128)(2,1)} %reshape.233) | data formatting | bytes 4194304 | tf_op jit(solution)/shard_map/while | solution.py:233
  514.2 250.8 %while.29 = (s32[]{:T(128)}, f32[8,2,512,2,64]{2,4,3,1,0:T(8,128)}, f32[8,2,512,2,64]{2,1,0,4,3:T(2,128)}, f32[8,2,512,2,64]{2,4,3,1,0:T(8,128)}, bf16[8,2,512,2...) while((s32[]{:T(128)}, f32[8,2,512,2,64]{2,4,3,1,0:T(8,128)}, ...), condition=%wide.region_25.26_spmd.clone, body=%wide.region_23.25_spmd.sunk.clone | while | flops 687609856 | bytes 52209824 | solution.py:233
  525.2 8.4 fusion.202
  533.6 7.2 fusion.203
  556.9 8.1 fusion.202
  565.0 7.1 fusion.203
  588.3 8.0 fusion.202
  596.4 7.1 fusion.203
  619.6 8.0 fusion.202
  627.6 7.1 fusion.203
  650.8 8.1 fusion.202
  658.9 7.1 fusion.203
  682.1 8.1 fusion.202
  690.2 7.1 fusion.203
  713.4 8.0 fusion.202
  721.4 7.1 fusion.203
  744.7 8.0 fusion.202
  752.7 7.1 fusion.203
  764.9 7.4 copy.75
  772.4 6.6 stack_reshape.11
  778.9 6.8 stack_reshape.10
  785.7 7.3 copy.73
  793.0 6.6 stack_reshape.9
  807.4 7.6 fusion.104
  815.1 10.3 %bitcast_convert_fusion = bf16[8192,512]{1,0:T(8,128)(2,1)} fusion(bf16[3,512,128]{1,2,0:T(8,128)(2,1)S(1)} %copy-done.9, f32[3]{0:T(128)S(1)} %copy-done.23, f32[1,8192,128]{1,2,0:T(8,128)} %stack_reshape.11, f32[1,8192,128]{1,2,0:T(8,128)} %stack_reshape.10, f32[1,8192,128]{1,2,0:T(8,128)} %stack_reshape.9, f32[3]{0:T(128)S(1)} %copy-done.27), kind=kOutput, calls=%fused_computation.76 | convolution fusion | flops 3239575552 | bytes 21364760 | tf_op jit(solution)/shard_map/ith,idh->td/dot_general | solution.py:257
  827.3 6.5 all-reduce
  833.9 10.7 %all-reduce.2 = (f32[512]{0:T(512)S(1)}, f32[512]{0:T(512)S(1)}, f32[512]{0:T(512)S(1)}, f32[512]{0:T(512)S(1)}, f32[512]{0:T(512)S(1)}, /*index=5*/f32[512]{0:T(512)S(1)}) all-reduce(f32[512]{0:T(512)S(1)} %get-tuple-element.292, f32[512]{0:T(512)S(1)} %get-tuple-element.220, ...), channel_id=1, replica_groups=mesh['dp'=8,'tensor'=4] {'tensor'}, use_global_device_ids=true, to_apply=%region_33.34 | all-reduce | flops 3072 | bytes 24576 | tf_op jit(solution)/shard_map/psum | solution.py:270
  844.6 37.4 %all-reduce.1 = (f32[512]{0:T(512)}, f32[512]{0:T(512)}, f32[512]{0:T(512)}, f32[512]{0:T(512)}, f32[512]{0:T(512)}, /*index=5*/f32[512]{0:T(512)}) all-reduce(f32[512]{0:T(512)S(1)} %get-tuple-element.274, f32[512]{0:T(512)S(1)} %get-tuple-element.275, f32[512]{0:T(512)S(1)} %get-tuple-element.276, ...), channel_id=1, replica_groups=mesh['dp'=8,'tensor'=4] {'dp'}, use_global_device_ids=true, to_apply=%region_34.35 | all-reduce | flops 3072 | bytes 24576 | tf_op jit(solution)/shard_map/psum | solution.py:269
  888.8 18.1 %all-reduce.4 = (bf16[2,128]{1,0:T(2,128)(2,1)}, bf16[512]{0:T(512)(128)(2,1)S(1)}) all-reduce(bf16[2,128]{1,0:T(2,128)(2,1)S(1)} %pad_maximum_fusion, bf16[512]{0:T(512)(128)(2,1)S(1)} %dynamic-slice.1), channel_id=1, replica_groups=mesh['dp'=8,'tensor'=4] {'dp'}, use_global_device_ids=true, to_apply=%region_30.31 | all-reduce | flops 768 | bytes 3072 | tf_op jit(solution)/shard_map/psum | solution.py:263
  920.1 59.6 %reduce-scatter.7.cloned.1.call-done = bf16[2048,512]{1,0:T(8,128)(2,1)} async-done(((bf16[8192,512]{1,0:T(8,128)(2,1)}), bf16[2048,512]{1,0:T(8,128)(2,1)}) %reduce-scatter.7.cloned.1.call-update) | async-done | bytes 2097168 | tf_op jit(solution)/shard_map/reduce_scatter | solution.py:31
  979.7 6.6 fusion.92
  (323 shorter events, 294.8 us)
Async XLA Ops:
  7.2 50.3 %copy-start.19 = (bf16[3,512,128]{2,1,0:T(8,128)(2,1)S(1)}, bf16[3,512,128]{2,1,0:T(8,128)(2,1)}, u32[]{:S(2)}) copy-start(bf16[3,512,128]{2,1,0:T(8,128)(2,1)} %param.23) | copy-start | bytes 1179652
  7.2 50.5 %copy-start.17 = (bf16[128,512]{1,0:T(8,128)(2,1)S(1)}, bf16[128,512]{1,0:T(8,128)(2,1)}, u32[]{:S(2)}) copy-start(bf16[128,512]{1,0:T(8,128)(2,1)} %param.25) | copy-start | bytes 393220
  7.2 108.7 %all-gather.6.cloned.1.call-start = ((), (), s32[]{:S(2)}) async-start(), calls=%async_computation.4 | async-start | bytes 10485760 | tf_op jit(solution)/shard_map/all_gather | solution.py:27
  9.8 48.7 %copy-start.10 = (bf16[512,512]{1,0:T(8,128)(2,1)S(1)}, bf16[512,512]{1,0:T(8,128)(2,1)}, u32[]{:S(2)}) copy-start(bf16[512,512]{1,0:T(8,128)(2,1)} %param.29) | copy-start | bytes 1572868
  9.8 48.7 %copy-start.12 = (bf16[512,512]{1,0:T(8,128)(2,1)S(1)}, bf16[512,512]{1,0:T(8,128)(2,1)}, u32[]{:S(2)}) copy-start(bf16[512,512]{1,0:T(8,128)(2,1)} %param.31) | copy-start | bytes 1572868
  52.6 13.9 %copy-start.38 = (bf16[2,128]{1,0:T(2,128)(2,1)S(1)}, bf16[2,128]{1,0:T(2,128)(2,1)}, u32[]{:S(2)}) copy-start(bf16[2,128]{1,0:T(2,128)(2,1)} %param.24) | copy-start | bytes 1540
  52.6 14.0 %copy-start.21 = (s32[16,512]{1,0:T(8,128)S(1)}, s32[16,512]{1,0:T(8,128)}, u32[]{:S(2)}) copy-start(s32[16,512]{1,0:T(8,128)} %param.21) | copy-start | bytes 98308
  52.6 14.0 %copy-start.37 = (s32[16]{0:T(128)S(1)}, s32[16]{0:T(128)}, u32[]{:S(2)}) copy-start(s32[16]{0:T(128)} %param.22) | copy-start | bytes 196
  57.4 242.3 %reduce-scatter.5.cloned.1.call-start = ((), (), s32[]{:S(2)}) async-start(), calls=%async_computation.5 | async-start | bytes 10485760 | tf_op jit(solution)/shard_map/reduce_scatter | solution.py:31
  57.7 64.4 %copy-start.8 = (bf16[3,512,128]{1,2,0:T(8,128)(2,1)}, bf16[3,512,128]{1,2,0:T(8,128)(2,1)S(1)}, u32[]{:S(2)}) copy-start(bf16[3,512,128]{1,2,0:T(8,128)(2,1)S(1)} %copy.65) | copy-start | bytes 1179652
  69.1 53.0 %copy-start.22 = (f32[3]{0:T(128)}, f32[3]{0:T(128)S(1)}, u32[]{:S(2)}) copy-start(f32[3]{0:T(128)S(1)} %get-tuple-element.301) | copy-start | bytes 40
  69.1 53.0 %copy-start.26 = (f32[3]{0:T(128)}, f32[3]{0:T(128)S(1)}, u32[]{:S(2)}) copy-start(f32[3]{0:T(128)S(1)} %get-tuple-element.302) | copy-start | bytes 40
  142.2 4.2 copy-start.5
  146.4 3.6 copy-start.6
  213.7 8.4 copy-start.20
  213.7 8.4 copy-start.29
  222.1 5.7 copy-start.2
  227.8 4.2 copy-start.30
  227.8 4.3 copy-start.31
  227.8 9.5 copy-start.32
  227.8 9.5 copy-start.33
  227.8 9.5 copy-start.34
  227.8 9.5 copy-start.35
  227.9 9.5 copy-start.36
  227.9 71.9 %copy-start = (bf16[2048,512]{1,0:T(8,128)(2,1)S(1)}, bf16[2048,512]{1,0:T(8,128)(2,1)}, u32[]{:S(2)}) copy-start(bf16[2048,512]{1,0:T(8,128)(2,1)} %param.20) | copy-start | bytes 6291460
  227.9 96.7 %all-gather.8.cloned.1.call-start = ((), (), s32[]{:S(2)}) async-start(), calls=%async_computation.6 | async-start | bytes 2621440 | tf_op jit(solution)/shard_map/all_gather | solution.py:182
  230.0 140.6 %all-gather.10.cloned.1.call-start = ((), (), s32[]{:S(2)}) async-start(), calls=%async_computation.7 | async-start | bytes 2621440 | tf_op jit(solution)/shard_map/all_gather | solution.py:184
  232.0 255.8 %all-gather.12.cloned.1.call-start = ((), (), s32[]{:S(2)}) async-start(), calls=%async_computation.8 | async-start | bytes 10485760 | tf_op jit(solution)/shard_map/all_gather | solution.py:27
  299.8 2.6 copy-start.3
  379.6 1.6 copy-start.7
  411.4 11.7 %copy-start.4 = (bf16[2048,512]{1,0:T(8,128)(2,1)S(1)}, bf16[2048,512]{1,0:T(8,128)(2,1)}, u32[]{:S(2)}) copy-start(bf16[2048,512]{1,0:T(8,128)(2,1)} %reduce-scatter.5.cloned.1.call-done) | copy-start | bytes 6291460
  425.4 2.0 copy-start.1
  429.3 385.7 %reduce-scatter.9.cloned.1.call-start = ((), (), s32[]{:S(2)}) async-start(), calls=%async_computation.10 | async-start | bytes 2621440 | tf_op jit(solution)/shard_map/reduce_scatter | solution.py:210
  443.0 372.1 %reduce-scatter.11.cloned.1.call-start = ((), (), s32[]{:S(2)}) async-start(), calls=%async_computation.11 | async-start | bytes 2621440 | tf_op jit(solution)/shard_map/reduce_scatter | solution.py:216
  443.1 44.7 %copy-start.18 = (bf16[128,512]{1,0:T(8,128)(2,1)S(1)}, bf16[128,512]{1,0:T(8,128)(2,1)}, u32[]{:S(2)}) copy-start(bf16[128,512]{1,0:T(8,128)(2,1)} %param.25) | copy-start | bytes 393220
  453.6 455.1 %all-reduce.8.cloned.1.call-start = ((), (), s32[]{:S(2)}) async-start(), calls=%async_computation.12 | async-start | bytes 3145728 | tf_op jit(solution)/shard_map/psum | solution.py:262
  799.7 6.1 copy-start.14
  799.7 6.5 copy-start.15
  799.7 7.7 copy-start.16
  799.7 7.7 copy-start.27
  807.4 7.7 copy-start.9
  807.4 7.7 copy-start.23
  815.1 164.7 %reduce-scatter.7.cloned.1.call-start = ((), (), s32[]{:S(2)}) async-start(), calls=%async_computation.9 | async-start | bytes 10485760 | tf_op jit(solution)/shard_map/reduce_scatter | solution.py:31
  825.4 8.5 copy-start.24
  825.4 8.5 copy-start.25
  825.4 8.5 copy-start.28
  884.6 30.4 %copy-start.11 = (bf16[512,512]{1,0:T(8,128)(2,1)S(1)}, bf16[512,512]{1,0:T(8,128)(2,1)}, u32[]{:S(2)}) copy-start(bf16[512,512]{1,0:T(8,128)(2,1)} %param.29) | copy-start | bytes 1572868
  884.6 32.9 %copy-start.13 = (bf16[512,512]{1,0:T(8,128)(2,1)S(1)}, bf16[512,512]{1,0:T(8,128)(2,1)}, u32[]{:S(2)}) copy-start(bf16[512,512]{1,0:T(8,128)(2,1)} %param.31) | copy-start | bytes 1572868
  (1 other events, 0.7 us)
Sparse Core Ops, SparseCore 0:
  57.6 58.2 all-gather.5
  228.0 71.7 reduce-scatter.4
  302.0 22.5 all-gather.7
  326.7 22.5 all-gather.9
  429.4 58.2 all-gather.11
  490.3 31.4 reduce-scatter.8
  524.3 31.4 reduce-scatter.10
  815.2 90.3 all-reduce.7
  908.4 71.3 reduce-scatter.6
